TPU v7x, 256 devices: a whole 4x4x8 slice. The times are simulated.
256 devices in a mesh: row: 64 (over x, z_lo, y, core), col: 4 (over z_hi).
Axes of the slice: x: 4, y: 4, z: 8 (z_hi: 4, z_lo: 2; z = z_hi * 2 + z_lo), core: 2. Of those that a mesh axis runs over, the one named last changes fastest.
Arguments:
- fields: float32 [4, 128, 512, 512], P(None, 'row', None, 'col'), may hold values from -6 to 6
- diffusivity: float32 [4], replicated, may hold values from 0.05 to 0.3
- records: float32 [6, 2097152], P(None, ('row', 'col')), may hold values from -6 to 6
- response_time: float32 [2097152], P(('row', 'col')), may hold values from 0.5 to 4
- cell_index: int32 [2097152], P(('row', 'col')), may hold values from 0 to 131071
- counts: int32 [256], P(('row', 'col')), may hold values from 4096 to 8192, as said below
- destination: int32 [2097152], P(('row', 'col')), may hold values from 0 to 4, as said below
- slot: int32 [2097152], P(('row', 'col')), may hold values from 0 to 255, as said below
Outputs:
- tendency: float32 [4, 128, 512, 512], P(None, 'row', None, 'col')
- kept: float32 [6, 2097152], P(None, ('row', 'col'))
- arrivals: float32 [4, 6, 65536], P(None, None, ('row', 'col'))
Inputs may be any that keep to these rules, and one draw needn't show every extreme that they name: `counts`: both wall rows of pencils are full. `destination`: only live particles leave; none leaves row index 0 downward or row index 63 upward. For each pencil and direction the leaving particles' slots are distinct; pencil 0 sends exactly 256 particles toward col index + 1; slot is 0 for particles that stay.
All inputs are finite; a program needn't handle non-finite values.
Results may differ from a plain program's by a relative error of at most 0.00009.
Values sent between devices are 32-bit elements; how exact they have to be, the bound alone decides.
A program may use at most 192 MiB of HBM per device.

v0:
```python
import math
import jax
import jax.numpy as jnp
from jax import lax
from jax.sharding import PartitionSpec as P

PART_DEV = 8192
MIG = 256
time_step = 0.2
coupling = 0.5
stretch = 1.5


def shifted(value, axis, steps):
    count = lax.axis_size(axis)
    first, last = (max(0, -steps), min(count, count - steps))
    return lax.ppermute(value, axis, [(source, source + steps) for source in range(first, last)])


def from_behind(block, axis, distance):
    devices = range(lax.axis_size(axis))
    route = [((i - distance) % len(devices), i) for i in devices]
    return lax.ppermute(block, axis, route)


def periodic_compact(points):
    index = jnp.arange(points, dtype=jnp.int32)
    offset = (index[None, :] - index[:, None]) % points
    lhs = jnp.where(offset == 0, 1.0, 0.0) + jnp.where(
        (offset == 1) | (offset == points - 1), 1.0 / 3.0, 0.0
    )
    rhs = jnp.where(offset == 1, 7.0 / 9.0, 0.0) - jnp.where(offset == points - 1, 7.0 / 9.0, 0.0)
    rhs = (
        rhs
        + jnp.where(offset == 2, 1.0 / 36.0, 0.0)
        - jnp.where(offset == points - 2, 1.0 / 36.0, 0.0)
    )
    factor = jnp.linalg.cholesky(lhs.astype(jnp.float32))
    return jax.scipy.linalg.cho_solve((factor, True), rhs.astype(jnp.float32))


def wall_compact(points):
    index = jnp.arange(points, dtype=jnp.int32)
    first = index == 0
    final = index == points - 1
    near = (index == 1) | (index == points - 2)
    lower = jnp.where(first, 0.0, jnp.where(final, 2.0, jnp.where(near, 0.25, 1.0 / 3.0))).astype(
        jnp.float32
    )
    upper = jnp.where(final, 0.0, jnp.where(first, 2.0, jnp.where(near, 0.25, 1.0 / 3.0))).astype(
        jnp.float32
    )
    middle = jnp.ones((points,), jnp.float32)
    offset = index[None, :] - index[:, None]
    inner = jnp.where(offset == 1, 7.0 / 9.0, 0.0) - jnp.where(offset == -1, 7.0 / 9.0, 0.0)
    inner = (
        inner + jnp.where(offset == 2, 1.0 / 36.0, 0.0) - jnp.where(offset == -2, 1.0 / 36.0, 0.0)
    )
    padde_rows = jnp.where(offset == 1, 0.75, 0.0) - jnp.where(offset == -1, 0.75, 0.0)
    top_row = (
        jnp.where(offset == 0, -2.5, 0.0)
        + jnp.where(offset == 1, 2.0, 0.0)
        + jnp.where(offset == 2, 0.5, 0.0)
    )
    end_row = (
        jnp.where(offset == 0, 2.5, 0.0)
        - jnp.where(offset == -1, 2.0, 0.0)
        - jnp.where(offset == -2, 0.5, 0.0)
    )
    rhs = jnp.where(
        first[:, None],
        top_row,
        jnp.where(final[:, None], end_row, jnp.where(near[:, None], padde_rows, inner)),
    )
    solved = lax.linalg.tridiagonal_solve(lower, middle, upper, rhs.astype(jnp.float32))
    coord = -1.0 + 2.0 * index.astype(jnp.float32) / (points - 1)
    slope = stretch * (1.0 - jnp.tanh(stretch * coord) ** 2) / math.tanh(stretch)
    return solved / slope[:, None]


def spectral_matrix(points):
    index = jnp.arange(points, dtype=jnp.int32)
    offset = index[:, None] - index[None, :]
    parity = (1 - 2 * (offset % 2)).astype(jnp.float32)
    angle = math.pi * offset.astype(jnp.float32) / points
    safe_angle = jnp.where(offset == 0, 1.0, angle)
    value = math.pi / points * parity * jnp.cos(safe_angle) / jnp.sin(safe_angle)
    return jnp.where(offset == 0, 0.0, value)


def spanwise_terms(pencil_data, viscous):
    highest = lax.Precision.HIGHEST
    deriv_z = spectral_matrix(pencil_data.shape[3])
    second_z = jnp.dot(deriv_z, deriv_z, precision=highest)
    along_z = jnp.einsum("ij,cabj->cabi", deriv_z, pencil_data, precision=highest)
    curve_z = jnp.einsum("ij,cabj->cabi", second_z, pencil_data, precision=highest)
    return -pencil_data[2] * along_z + viscous * curve_z


def on_device(fields, diffusivity, records, response_time, cell_index, counts, destination, slot):
    highest = lax.Precision.HIGHEST
    viscous = diffusivity[:, None, None, None]
    planes = fields.shape[2]
    deriv_x = periodic_compact(planes)
    second_x = jnp.dot(deriv_x, deriv_x, precision=highest)
    along_x = jnp.einsum("ij,cyjz->cyiz", deriv_x, fields, precision=highest)
    curve_x = jnp.einsum("ij,cyjz->cyiz", second_x, fields, precision=highest)
    partial_x = -fields[0] * along_x + viscous * curve_x
    local = jnp.arange(PART_DEV, dtype=jnp.int32)
    live = local < counts[0]
    flat_speed = fields[0:3].reshape(3, -1)
    fluid = jnp.take(flat_speed, cell_index, axis=1)
    drag = (fluid - records[3:6]) / response_time
    velocity = records[3:6] + time_step * drag
    moved_pos = records[0:3] + time_step * velocity
    moved = jnp.concatenate([moved_pos, velocity], axis=0)
    force = jnp.where(live[None, :], -coupling * drag, 0.0)
    deposit = (
        jnp.zeros_like(flat_speed)
        .at[:, cell_index]
        .add(force)
        .reshape(3, fields.shape[1], fields.shape[2], fields.shape[3])
    )
    partial_x = partial_x.at[0:3].add(deposit)
    normal_pencil = lax.all_to_all(fields, "row", split_axis=2, concat_axis=1, tiled=True)
    deriv_y = wall_compact(normal_pencil.shape[1])
    second_y = jnp.dot(deriv_y, deriv_y, precision=highest)
    along_y = jnp.einsum("ij,cjxz->cixz", deriv_y, normal_pencil, precision=highest)
    curve_y = jnp.einsum("ij,cjxz->cixz", second_y, normal_pencil, precision=highest)
    partial_y = -normal_pencil[1] * along_y + viscous * curve_y
    span_pencil = lax.all_to_all(normal_pencil, "col", split_axis=1, concat_axis=3, tiled=True)
    partial_z = spanwise_terms(span_pencil, viscous)
    partial_y = partial_y + lax.all_to_all(
        partial_z, "col", split_axis=3, concat_axis=1, tiled=True
    )
    tendency = partial_x + lax.all_to_all(partial_y, "row", split_axis=1, concat_axis=2, tiled=True)
    staying = live & (destination == 0)
    kept = jnp.where(staying[None, :], moved, 0.0)
    leaving = live & (destination > 0)
    target = jnp.where(leaving, (destination - 1) * MIG + slot, 4 * MIG)
    outgoing = (
        jnp.zeros((6, 4 * MIG + 1), jnp.float32)
        .at[:, target]
        .add(jnp.where(leaving[None, :], moved, 0.0))
    )
    outgoing = outgoing[:, : 4 * MIG].reshape(6, 4, MIG)
    received = []
    for direction, offset in ((0, 1), (1, -1)):
        received.append(shifted(outgoing[:, direction], "row", offset))
    for direction, offset in ((2, 1), (3, -1)):
        received.append(from_behind(outgoing[:, direction], "col", offset))
    arrivals = jnp.stack(received, axis=0)
    return (tendency, kept, arrivals)


def solution(mesh):
    return jax.shard_map(
        on_device,
        mesh=mesh,
        in_specs=(
            P(None, "row", None, "col"),
            P(),
            P(None, ("row", "col")),
            P(("row", "col")),
            P(("row", "col")),
            P(("row", "col")),
            P(("row", "col")),
            P(("row", "col")),
        ),
        out_specs=(
            P(None, "row", None, "col"),
            P(None, ("row", "col")),
            P(None, None, ("row", "col")),
        ),
        check_vma=False,
    )
```

profile of v0, /device:TPU:1, one launch (start us, length us, event | category | flops | bytes accessed | tf_op | source)
XLA Modules:
  0.0 1095.8 jit_solution(8864007310958328743)
XLA Ops:
  0.6 4.3 copy.115
  4.9 10.5 all-to-all-start
  16.9 30.5 %copy.111 = f32[3,2,512,128]{0,3,2,1:T(8,128)} copy(f32[3,2,512,128]{3,2,1,0:T(8,128)S(1)} %slice-done) | data formatting | bytes 3145728 | tf_op jit(solution)/shard_map/slice | solution.py:111
  47.3 118.4 %gather_fusion = f32[8192,3]{1,0:T(8,128)} fusion(f32[3,131072]{0,1:T(8,128)} %bitcast.277, s32[8192]{0:T(1024)S(1)} %get-tuple-element.480), kind=kCustom, calls=%fused_computation | custom fusion | bytes 229376 | tf_op jit(solution)/shard_map/jit(_take)/gather | solution.py:112
  165.7 2.9 copy.112
  170.3 2.7 copy.126
  173.0 53.6 %scatter_custom_fusion.1 = f32[6,1025]{0,1:T(8,128)S(1)} fusion(s32[8192]{0:T(1024)S(1)} %compare_select_fusion, f32[8192,6]{1,0:T(8,128)} %copy.126, f32[]{:T(128)} %constant.319.clone.1), kind=kCustom, calls=%fused_computation.317 | custom fusion | flops 49152 | bytes 25112 | tf_op jit(solution)/shard_map/scatter-add | solution.py:144
  226.8 4.2 collective-permute-start.3
  232.4 5.2 collective-permute-start.1
  242.7 194.9 %while.34 = (s32[]{:T(128)}, f32[]{:T(128)}, f32[128]{0:T(128)S(1)}, f32[3,32]{1,0:T(4,128)S(1)}, f32[3,32,128]{2,1,0:T(8,128)S(1)}, /*index=5*/f32[3,32]{1,0:T(...) while((s32[]{:T(128)}, f32[]{:T(128)}, ...), condition=%wide.region_10.11_spmd, body=%wide.region_9.10_spmd.sunk | while | flops 12417 | bytes 103669 | solution.py:75
  286.5 20.2 %fusion.526 = (f32[128]{0:T(128)S(1)}, f32[128]{0:T(128)S(1)}, f32[128]{0:T(128)S(1)}, f32[128]{0:T(128)S(1)}, f32[128]{0:T(128)S(1)}, /*index=5*/f32[128]{0:T(1...) fusion(f32[3,32,128]{2,1,0:T(8,128)S(1)} %get-tuple-element.112, ...), kind=kLoop, calls=%fused_computation.44.clone.1 | loop fusion | flops 12288 | bytes 33664 | tf_op jit(solution)/shard_map/while/body/eval_jaxpr/div | solution.py:75
  351.4 20.2 %fusion.526 = (f32[128]{0:T(128)S(1)}, f32[128]{0:T(128)S(1)}, f32[128]{0:T(128)S(1)}, f32[128]{0:T(128)S(1)}, f32[128]{0:T(128)S(1)}, /*index=5*/f32[128]{0:T(1...) fusion(f32[3,32,128]{2,1,0:T(8,128)S(1)} %get-tuple-element.112, ...), kind=kLoop, calls=%fused_computation.44.clone.1 | loop fusion | flops 12288 | bytes 33664 | tf_op jit(solution)/shard_map/while/body/eval_jaxpr/div | solution.py:75
  416.2 20.2 %fusion.526 = (f32[128]{0:T(128)S(1)}, f32[128]{0:T(128)S(1)}, f32[128]{0:T(128)S(1)}, f32[128]{0:T(128)S(1)}, f32[128]{0:T(128)S(1)}, /*index=5*/f32[128]{0:T(1...) fusion(f32[3,32,128]{2,1,0:T(8,128)S(1)} %get-tuple-element.112, ...), kind=kLoop, calls=%fused_computation.44.clone.1 | loop fusion | flops 12288 | bytes 33664 | tf_op jit(solution)/shard_map/while/body/eval_jaxpr/div | solution.py:75
  441.4 11.7 %cholesky.104 = f32[128,128]{1,0:T(8,128)S(1)} custom-call(f32[128,128]{1,0:T(8,128)S(1)} %cholesky.266), custom_call_target="Cholesky" | custom-call | tf_op jit(solution)/shard_map/jit(cholesky)/cholesky | solution.py:38
  453.3 9.8 custom-call.34
  463.7 11.7 %cholesky.217 = f32[128,128]{1,0:T(8,128)S(1)} custom-call(f32[128,128]{1,0:T(8,128)S(1)} %cholesky.270), custom_call_target="Cholesky" | custom-call | tf_op jit(solution)/shard_map/jit(cholesky)/cholesky | solution.py:38
  475.5 10.0 custom-call.35
  486.1 11.7 %cholesky.238 = f32[128,128]{1,0:T(8,128)S(1)} custom-call(f32[128,128]{1,0:T(8,128)S(1)} %cholesky.275), custom_call_target="Cholesky" | custom-call | tf_op jit(solution)/shard_map/jit(cholesky)/cholesky | solution.py:38
  497.9 9.8 custom-call.36
  508.3 11.7 %cholesky.255 = f32[128,128]{1,0:T(8,128)S(1)} custom-call(f32[128,128]{1,0:T(8,128)S(1)} %convolution_subtract_fusion.8), custom_call_target="Cholesky" | custom-call | tf_op jit(solution)/shard_map/jit(cholesky)/cholesky | solution.py:38
  560.4 19.7 %fusion.304 = (f32[128]{0:T(128)S(1)}, f32[128]{0:T(128)S(1)}, f32[128]{0:T(128)S(1)}, f32[128]{0:T(128)S(1)}, f32[128]{0:T(128)S(1)}, /*index=5*/f32[128]{0:T(1...) fusion(f32[128,128]{1,0:T(8,128)S(1)} %select_select_fusion.1, ...), kind=kLoop, calls=%fused_computation.488 | loop fusion | flops 11904 | bytes 32504 | tf_op jit(solution)/shard_map/eval_jaxpr/div | solution.py:75
  584.4 6.5 sort
  591.0 65.7 %while.35 = (s32[]{:T(128)}, f32[128]{0:T(128)S(1)}, f32[3,32,128]{2,1,0:T(8,128)S(1)}, f32[3,32,128]{2,1,0:T(8,128)S(1)}, f32[3,32]{1,0:T(4,128)S(1)}, /*index=...) while((s32[]{:T(128)}, f32[128]{0:T(128)S(1)}, ...), condition=%wide.region_12.13_spmd, body=%wide.region_11.12_spmd.sunk | while | flops 8226 | bytes 101341 | solution.py:75
  592.4 20.3 %fusion.529 = (f32[128]{0:T(128)S(1)}, f32[128]{0:T(128)S(1)}, f32[128]{0:T(128)S(1)}, f32[128]{0:T(128)S(1)}, f32[128]{0:T(128)S(1)}, /*index=5*/f32[128]{0:T(1...) fusion(f32[3,32,128]{2,1,0:T(8,128)S(1)} %get-tuple-element.123, ...), kind=kLoop, calls=%fused_computation.172.clone.1 | loop fusion | flops 8192 | bytes 33536 | tf_op jit(solution)/shard_map/while/body/eval_jaxpr/sub | solution.py:75
  614.3 20.3 %fusion.529 = (f32[128]{0:T(128)S(1)}, f32[128]{0:T(128)S(1)}, f32[128]{0:T(128)S(1)}, f32[128]{0:T(128)S(1)}, f32[128]{0:T(128)S(1)}, /*index=5*/f32[128]{0:T(1...) fusion(f32[3,32,128]{2,1,0:T(8,128)S(1)} %get-tuple-element.123, ...), kind=kLoop, calls=%fused_computation.172.clone.1 | loop fusion | flops 8192 | bytes 33536 | tf_op jit(solution)/shard_map/while/body/eval_jaxpr/sub | solution.py:75
  636.2 20.3 %fusion.529 = (f32[128]{0:T(128)S(1)}, f32[128]{0:T(128)S(1)}, f32[128]{0:T(128)S(1)}, f32[128]{0:T(128)S(1)}, f32[128]{0:T(128)S(1)}, /*index=5*/f32[128]{0:T(1...) fusion(f32[3,32,128]{2,1,0:T(8,128)S(1)} %get-tuple-element.123, ...), kind=kLoop, calls=%fused_computation.172.clone.1 | loop fusion | flops 8192 | bytes 33536 | tf_op jit(solution)/shard_map/while/body/eval_jaxpr/sub | solution.py:75
  658.4 3.3 fusion.368
  661.7 3.3 fusion.367
  665.0 3.2 fusion.366
  668.2 3.1 fusion.365
  671.3 3.1 fusion.364
  674.5 3.1 fusion.363
  677.5 3.2 fusion.362
  680.8 3.3 fusion.361
  684.1 7.0 convolution_bitcast_fusion
  691.2 2.7 copy.148
  696.4 5.4 all-to-all-start.1
  701.9 10.2 while.36
  712.2 38.1 %all-to-all-done.1 = f32[4,128,8,128]{3,2,0,1:T(8,128)} async-done(((f32[4,128,8,128]{3,2,0,1:T(8,128)}), f32[4,128,8,128]{3,2,0,1:T(8,128)}, u32[]{:S(2)}, u32[]{:S(2)}) %all-to-all-start.1) | async-done | bytes 2097184 | tf_op jit(solution)/shard_map/all_to_all | solution.py:131
  750.3 4.3 copy.121
  754.6 3.1 all_to_all.59
  761.0 3.5 fusion.493
  764.6 9.0 bitcast_add_fusion.2
  773.6 8.4 copy.122
  782.0 7.3 reshape.572
  789.3 4.5 all-to-all-start.2
  793.8 2.7 fusion.360
  796.4 40.7 %custom-call.37 = f32[4,128,128]{1,2,0:T(8,128)} custom-call(f32[4,128,128]{2,1,0:T(8,128)} %get-tuple-element.177), custom_call_target="InvertDiagBlocksLowerTriangular" | custom-call | tf_op jit(solution)/shard_map/jit(_cho_solve)/triangular_solve | solution.py:39
  837.2 2.7 copy.113
  839.8 121.9 %scatter_custom_fusion = f32[3,131072]{0,1:T(8,128)} fusion(s32[8192]{0:T(1024)} %get-tuple-element.196, f32[]{:T(128)} %constant.319.clone.1, f32[8192,3]{1,0:T(8,128)} %copy.113, s32[8192]{0:T(1024)S(1)} %broadcast_clamp_fusion), kind=kCustom, calls=%fused_computation.235 | custom fusion | flops 24576 | bytes 1573376 | tf_op jit(solution)/shard_map/scatter-add | solution.py:121
  961.8 36.1 %copy.138 = f32[3,2,512,128]{3,2,1,0:T(8,128)} copy(f32[3,2,512,128]{0,3,2,1:T(8,128)} %bitcast.280) | data formatting | bytes 3145728 | tf_op jit(solution)/shard_map/reshape.84
  1000.6 2.6 fusion.358
  1003.2 2.7 fusion.357
  1005.9 2.7 fusion.356
  1018.8 3.2 fusion.226
  1022.6 9.0 reduce.26
  1031.5 7.8 reshape.573
  1039.3 6.3 copy.123
  1045.6 4.5 bitcast_add_fusion.1
  1052.6 11.0 %all-to-all-start.3 = ((f32[4,128,8,128]{3,2,0,1:T(8,128)}), f32[4,128,8,128]{3,2,0,1:T(8,128)}, u32[]{:S(2)}, u32[]{:S(2)}) async-start(f32[4,128,8,128]{3,2,0,1:T(8,128)} %copy.124), calls=%async_computation.3 | async-start | bytes 4194304 | tf_op jit(solution)/shard_map/all_to_all | solution.py:136
  1070.6 3.6 fusion.492
  1074.2 3.7 bitcast_add_fusion.3
  1079.7 12.5 %all-to-all-done.3 = f32[4,128,8,128]{3,2,0,1:T(8,128)} async-done(((f32[4,128,8,128]{3,2,0,1:T(8,128)}), f32[4,128,8,128]{3,2,0,1:T(8,128)}, u32[]{:S(2)}, u32[]{:S(2)}) %all-to-all-start.3) | async-done | bytes 2097184 | tf_op jit(solution)/shard_map/all_to_all | solution.py:136
  1092.3 3.1 bitcast_add_fusion
  (216 shorter events, 74.4 us)
Async XLA Ops:
  4.9 686.3 %all-to-all-start = ((f32[4,2,512,128]{3,0,1,2:T(4,128)}), f32[4,2,512,128]{3,0,1,2:T(4,128)}, u32[]{:S(2)}, u32[]{:S(2)}) async-start(f32[4,2,512,128]{3,0,1,2:T(4,128)} %copy.115), calls=%async_computation | async-start | bytes 4194304 | tf_op jit(solution)/shard_map/all_to_all | solution.py:125
  15.4 0.8 copy-start.10
  15.4 1.4 slice-start
  165.7 3.6 copy-start.11
  165.7 3.6 copy-start.9
  165.7 3.6 copy-start.12
  170.3 2.7 copy-start.13
  226.8 851.6 %collective-permute-start.3 = (f32[6,256]{1,0:T(8,128)S(1)}, f32[6,256]{1,0:T(8,128)}, u32[]{:S(2)}, u32[]{:S(2)}) collective-permute-start(f32[6,256]{1,0:T(8,128)S(1)} %bitcast.1864), channel_id=1, source_target_pairs={{1,0},{2,1},{3,2},{0,3},{5,4},{6,5},{7,6},{4,7},{9,8},{10,9},{11,1... | collective-permute-start | bytes 18440 | tf_op jit(solution)/shard_map/ppermute | solution.py:23
  231.7 846.7 %collective-permute-start.2 = (f32[6,256]{1,0:T(8,128)}, f32[6,256]{1,0:T(8,128)}, u32[]{:S(2)}, u32[]{:S(2)}) collective-permute-start(f32[6,256]{1,0:T(8,128)} %bitcast.568), channel_id=1, source_target_pairs={{3,0},{0,1},{1,2},{2,3},{7,4},{4,5},{5,6},{6,7},{11,8},{8,9},{9,10... | collective-permute-start | bytes 18440 | tf_op jit(solution)/shard_map/ppermute | solution.py:23
  232.4 846.0 %collective-permute-start.1 = (f32[6,256]{1,0:T(8,128)}, f32[6,256]{1,0:T(8,128)}, u32[]{:S(2)}, u32[]{:S(2)}) collective-permute-start(f32[6,256]{1,0:T(8,128)} %bitcast.566), channel_id=1, source_target_pairs={{4,0},{8,4},{12,8},{16,12},{20,16},{24,20},{28,24},{32,28},{36,32}... | collective-permute-start | bytes 18440 | tf_op jit(solution)/shard_map/ppermute | solution.py:17
  238.3 840.1 %collective-permute-start = (f32[6,256]{1,0:T(8,128)}, f32[6,256]{1,0:T(8,128)}, u32[]{:S(2)}, u32[]{:S(2)}) collective-permute-start(f32[6,256]{1,0:T(8,128)} %bitcast.564), channel_id=1, source_target_pairs={{0,4},{4,8},{8,12},{12,16},{16,20},{20,24},{24,28},{28,32},{32,36}... | collective-permute-start | bytes 18440 | tf_op jit(solution)/shard_map/ppermute | solution.py:17
  437.7 219.0 %copy-start.8 = (f32[3,32,128]{2,1,0:T(8,128)}, f32[3,32,128]{2,1,0:T(8,128)S(1)}, u32[]{:S(2)}) copy-start(f32[3,32,128]{2,1,0:T(8,128)S(1)} %get-tuple-element.164) | copy-start | bytes 147460
  696.4 5.4 copy-start.24
  696.4 53.9 %all-to-all-start.1 = ((f32[4,128,8,128]{3,2,0,1:T(8,128)}), f32[4,128,8,128]{3,2,0,1:T(8,128)}, u32[]{:S(2)}, u32[]{:S(2)}) async-start(f32[4,128,8,128]{3,2,0,1:T(8,128)} %copy.117), calls=%async_computation.1 | async-start | bytes 4194304 | tf_op jit(solution)/shard_map/all_to_all | solution.py:131
  757.6 2.2 copy-start.6
  759.4 1.6 copy-start.1
  761.0 3.5 copy-start.14
  789.3 232.7 %all-to-all-start.2 = ((f32[4,1,131072]{2,1,0:T(1,128)}), f32[4,1,131072]{2,1,0:T(1,128)}, u32[]{:S(2)}, u32[]{:S(2)}) async-start(f32[4,1,131072]{2,1,0:T(1,128)} %reshape.572), calls=%async_computation.2 | async-start | bytes 4194304 | tf_op jit(solution)/shard_map/all_to_all | solution.py:133
  961.8 51.3 %copy-start.15 = (f32[1,128]{1,0:T(1,128)S(1)}, f32[1,128]{1,0:T(1,128)}, u32[]{:S(2)}) copy-start(f32[1,128]{1,0:T(1,128)} %get-tuple-element.299) | copy-start | bytes 1540
  961.8 51.3 %copy-start.16 = (f32[1,128]{1,0:T(1,128)S(1)}, f32[1,128]{1,0:T(1,128)}, u32[]{:S(2)}) copy-start(f32[1,128]{1,0:T(1,128)} %get-tuple-element.301) | copy-start | bytes 1540
  961.8 51.3 %copy-start.17 = (f32[1,128]{1,0:T(1,128)S(1)}, f32[1,128]{1,0:T(1,128)}, u32[]{:S(2)}) copy-start(f32[1,128]{1,0:T(1,128)} %get-tuple-element.303) | copy-start | bytes 1540
  961.8 51.3 %copy-start.18 = (f32[1,128]{1,0:T(1,128)S(1)}, f32[1,128]{1,0:T(1,128)}, u32[]{:S(2)}) copy-start(f32[1,128]{1,0:T(1,128)} %get-tuple-element.305) | copy-start | bytes 1540
  961.8 51.3 %copy-start.19 = (f32[1,128]{1,0:T(1,128)S(1)}, f32[1,128]{1,0:T(1,128)}, u32[]{:S(2)}) copy-start(f32[1,128]{1,0:T(1,128)} %get-tuple-element.307) | copy-start | bytes 1540
  961.8 51.3 %copy-start.20 = (f32[1,128]{1,0:T(1,128)S(1)}, f32[1,128]{1,0:T(1,128)}, u32[]{:S(2)}) copy-start(f32[1,128]{1,0:T(1,128)} %get-tuple-element.309) | copy-start | bytes 1540
  961.8 51.3 %copy-start.21 = (f32[1,128]{1,0:T(1,128)S(1)}, f32[1,128]{1,0:T(1,128)}, u32[]{:S(2)}) copy-start(f32[1,128]{1,0:T(1,128)} %get-tuple-element.311) | copy-start | bytes 1540
  961.8 51.3 %copy-start.22 = (f32[1,128]{1,0:T(1,128)S(1)}, f32[1,128]{1,0:T(1,128)}, u32[]{:S(2)}) copy-start(f32[1,128]{1,0:T(1,128)} %get-tuple-element.313) | copy-start | bytes 1540
  961.8 51.3 %copy-start.23 = (f32[1,128]{1,0:T(1,128)S(1)}, f32[1,128]{1,0:T(1,128)}, u32[]{:S(2)}) copy-start(f32[1,128]{1,0:T(1,128)} %get-tuple-element.315) | copy-start | bytes 1540
  1014.0 1.4 copy-start.3
  1052.6 11.0 %copy-start.4 = (f32[512,512]{1,0:T(8,128)S(1)}, f32[512,512]{1,0:T(8,128)}, u32[]{:S(2)}) copy-start(f32[512,512]{1,0:T(8,128)} %copy-done.3) | copy-start | bytes 3145732
  1052.6 11.0 %copy-start.5 = (f32[128,512]{1,0:T(8,128)S(1)}, f32[128,512]{1,0:T(8,128)}, u32[]{:S(2)}) copy-start(f32[128,512]{1,0:T(8,128)} %fusion.238) | copy-start | bytes 786436
  1052.6 11.4 %copy-start.7 = (f32[4,128,128]{1,2,0:T(8,128)S(1)}, f32[4,128,128]{1,2,0:T(8,128)}, u32[]{:S(2)}) copy-start(f32[4,128,128]{1,2,0:T(8,128)} %custom-call.37) | copy-start | bytes 786436
  1052.6 39.6 %all-to-all-start.3 = ((f32[4,128,8,128]{3,2,0,1:T(8,128)}), f32[4,128,8,128]{3,2,0,1:T(8,128)}, u32[]{:S(2)}, u32[]{:S(2)}) async-start(f32[4,128,8,128]{3,2,0,1:T(8,128)} %copy.124), calls=%async_computation.3 | async-start | bytes 4194304 | tf_op jit(solution)/shard_map/all_to_all | solution.py:136
  1067.6 2.9 copy-start
  1074.2 3.7 copy-start.2
where the time goes:
time: 1110 us; the launch traced here: 1100 us
  other arithmetic  505 us (45%)
  local copies, waits for them, and re-layouts  281 us (25%)
  loops' own time  125 us (11%)
  waiting for transfers between devices  50.7 us (5%)
  matrix products  47.3 us (4%)
  between operations  44 us (4%)
  starting transfers between devices  42.7 us (4%)
    scatter-add x3, other arithmetic, on_device(): deposit = jnp.zeros_like(flat_speed).at[:, cell_index].add(force).reshape...  129 us
    another operation x2, loops' own time, wall_compact(): lax.linalg.tridiagonal_solve(lower, middle, upper, rhs.astype(jnp.float32))  125 us
    gather x2, local copies, waits for them, and re-layouts, on_device(): fluid = jnp.take(flat_speed, cell_index, axis=1)  121 us
    div x4, other arithmetic, wall_compact(): lax.linalg.tridiagonal_solve(lower, middle, upper, rhs.astype(jnp.float32))  80.3 us
    another operation x14, other arithmetic, periodic_compact(): factor = jnp.linalg.cholesky(lhs.astype(jnp.float32))  78.7 us
    sub x3, other arithmetic, wall_compact(): lax.linalg.tridiagonal_solve(lower, middle, upper, rhs.astype(jnp.float32))  61 us
    scatter-add x1, other arithmetic, on_device(): outgoing = jnp.zeros((6, 4 * MIG + 1), jnp.float32).at[:, target].add(jnp...  53.6 us
    another operation x15, local copies, waits for them, and re-layouts  46.3 us
  transfers between devices with their start and end apart: 8, of which 2 were waited for; matrix products, arithmetic and copies ran while one was open for 75% of the time, Pallas kernels for 0%

commit v1 on v0

--- a/solution.py
+++ b/solution.py
@@ -3,6 +3,7 @@
 import jax.numpy as jnp
 from jax import lax
 from jax.sharding import PartitionSpec as P
+from jax.lax import all_to_all, psum
 
 PART_DEV = 8192
 MIG = 256
@@ -130,9 +131,16 @@
     partial_y = -normal_pencil[1] * along_y + viscous * curve_y
     span_pencil = lax.all_to_all(normal_pencil, "col", split_axis=1, concat_axis=3, tiled=True)
     partial_z = spanwise_terms(span_pencil, viscous)
-    partial_y = partial_y + lax.all_to_all(
-        partial_z, "col", split_axis=3, concat_axis=1, tiled=True
+    report_orders = lambda piece_in, dim_i, where_dim: jnp.concatenate(
+        all_to_all(
+            jnp.stack(jnp.split(piece_in, psum(1, axis_name="col"), axis=dim_i)),
+            axis_name="col",
+            split_axis=0,
+            concat_axis=0,
+        ),
+        axis=where_dim,
     )
+    partial_y = partial_y + report_orders(partial_z, 3, 1)
     tendency = partial_x + lax.all_to_all(partial_y, "row", split_axis=1, concat_axis=2, tiled=True)
     staying = live & (destination == 0)
     kept = jnp.where(staying[None, :], moved, 0.0)

time: 1110 us -> 1070 us (0.964)
  local copies, waits for them, and re-layouts: 281 us -> 254 us
    unnamed x58 -> x60, local copies, waits for them, and re-layouts: 24.1 us -> 9.41 us
    another operation x15 -> x16, local copies, waits for them, and re-layouts: 46.3 us -> 47.2 us
  transfers between devices with their start and end apart: 8 -> 8, of which waited for: 2 -> 2; matrix products, arithmetic and copies ran while one was open for 75% -> 74% of each run, Pallas kernels for 0% -> 0%
where the time goes in v1:
time: 1070 us; the launch traced here: 1060 us
  other arithmetic  498 us (47%)
  local copies, waits for them, and re-layouts  254 us (24%)
  loops' own time  124 us (12%)
  waiting for transfers between devices  50.3 us (5%)
  between operations  44.3 us (4%)
  matrix products  44 us (4%)
  starting transfers between devices  41.1 us (4%)
    scatter-add x3, other arithmetic, on_device(): deposit = jnp.zeros_like(flat_speed).at[:, cell_index].add(force).reshape...  128 us
    another operation x2, loops' own time, wall_compact(): lax.linalg.tridiagonal_solve(lower, middle, upper, rhs.astype(jnp.float32))  124 us
    gather x2, local copies, waits for them, and re-layouts, on_device(): fluid = jnp.take(flat_speed, cell_index, axis=1)  121 us
    div x4, other arithmetic, wall_compact(): lax.linalg.tridiagonal_solve(lower, middle, upper, rhs.astype(jnp.float32))  79.8 us
    another operation x14, other arithmetic, periodic_compact(): factor = jnp.linalg.cholesky(lhs.astype(jnp.float32))  79 us
    sub x3, other arithmetic, wall_compact(): lax.linalg.tridiagonal_solve(lower, middle, upper, rhs.astype(jnp.float32))  61 us
    scatter-add x1, other arithmetic, on_device(): outgoing = jnp.zeros((6, 4 * MIG + 1), jnp.float32).at[:, target].add(jnp...  53.6 us
    another operation x15, local copies, waits for them, and re-layouts  47 us
  transfers between devices with their start and end apart: 8, of which 2 were waited for; matrix products, arithmetic and copies ran while one was open for 74% of the time, Pallas kernels for 0%

profile of v1, /device:TPU:1, one launch (start us, length us, event | category | flops | bytes accessed | tf_op | source)
XLA Modules:
  0.0 1055.3 jit_solution(10082964858229339219)
XLA Ops:
  0.6 4.3 copy.112
  4.9 10.5 all-to-all-start
  16.9 30.5 %copy.108 = f32[3,2,512,128]{0,3,2,1:T(8,128)} copy(f32[3,2,512,128]{3,2,1,0:T(8,128)S(1)} %slice-done) | data formatting | bytes 3145728 | tf_op jit(solution)/shard_map/slice | solution.py:112
  47.4 118.6 %gather_fusion = f32[8192,3]{1,0:T(8,128)} fusion(f32[3,131072]{0,1:T(8,128)} %bitcast.277, s32[8192]{0:T(1024)S(1)} %get-tuple-element.484), kind=kCustom, calls=%fused_computation | custom fusion | bytes 229376 | tf_op jit(solution)/shard_map/jit(_take)/gather | solution.py:113
  166.0 2.9 copy.109
  170.5 2.7 copy.122
  173.2 53.6 %scatter_custom_fusion.1 = f32[6,1025]{0,1:T(8,128)S(1)} fusion(s32[8192]{0:T(1024)S(1)} %compare_select_fusion, f32[8192,6]{1,0:T(8,128)} %copy.122, f32[]{:T(128)} %constant.319.clone.1), kind=kCustom, calls=%fused_computation.322 | custom fusion | flops 49152 | bytes 25112 | tf_op jit(solution)/shard_map/scatter-add | solution.py:152
  227.0 4.1 collective-permute-start.3
  232.5 5.3 collective-permute-start.1
  242.8 193.3 %while.34 = (s32[]{:T(128)}, f32[]{:T(128)}, f32[128]{0:T(128)S(1)}, f32[3,32]{1,0:T(4,128)S(1)}, f32[3,32,128]{2,1,0:T(8,128)S(1)}, /*index=5*/f32[3,32]{1,0:T(...) while((s32[]{:T(128)}, f32[]{:T(128)}, ...), condition=%wide.region_10.11_spmd, body=%wide.region_9.10_spmd.sunk | while | flops 12417 | bytes 103669 | solution.py:76
  286.3 20.1 %fusion.526 = (f32[128]{0:T(128)S(1)}, f32[128]{0:T(128)S(1)}, f32[128]{0:T(128)S(1)}, f32[128]{0:T(128)S(1)}, f32[128]{0:T(128)S(1)}, /*index=5*/f32[128]{0:T(1...) fusion(f32[3,32,128]{2,1,0:T(8,128)S(1)} %get-tuple-element.112, ...), kind=kLoop, calls=%fused_computation.44.clone.1 | loop fusion | flops 12288 | bytes 33664 | tf_op jit(solution)/shard_map/while/body/eval_jaxpr/div | solution.py:76
  350.7 20.1 %fusion.526 = (f32[128]{0:T(128)S(1)}, f32[128]{0:T(128)S(1)}, f32[128]{0:T(128)S(1)}, f32[128]{0:T(128)S(1)}, f32[128]{0:T(128)S(1)}, /*index=5*/f32[128]{0:T(1...) fusion(f32[3,32,128]{2,1,0:T(8,128)S(1)} %get-tuple-element.112, ...), kind=kLoop, calls=%fused_computation.44.clone.1 | loop fusion | flops 12288 | bytes 33664 | tf_op jit(solution)/shard_map/while/body/eval_jaxpr/div | solution.py:76
  415.0 20.1 %fusion.526 = (f32[128]{0:T(128)S(1)}, f32[128]{0:T(128)S(1)}, f32[128]{0:T(128)S(1)}, f32[128]{0:T(128)S(1)}, f32[128]{0:T(128)S(1)}, /*index=5*/f32[128]{0:T(1...) fusion(f32[3,32,128]{2,1,0:T(8,128)S(1)} %get-tuple-element.112, ...), kind=kLoop, calls=%fused_computation.44.clone.1 | loop fusion | flops 12288 | bytes 33664 | tf_op jit(solution)/shard_map/while/body/eval_jaxpr/div | solution.py:76
  439.8 11.7 %cholesky.104 = f32[128,128]{1,0:T(8,128)S(1)} custom-call(f32[128,128]{1,0:T(8,128)S(1)} %cholesky.266), custom_call_target="Cholesky" | custom-call | tf_op jit(solution)/shard_map/jit(cholesky)/cholesky | solution.py:39
  451.7 9.8 custom-call.34
  462.2 11.7 %cholesky.217 = f32[128,128]{1,0:T(8,128)S(1)} custom-call(f32[128,128]{1,0:T(8,128)S(1)} %cholesky.270), custom_call_target="Cholesky" | custom-call | tf_op jit(solution)/shard_map/jit(cholesky)/cholesky | solution.py:39
  473.9 10.3 custom-call.35
  484.8 11.7 %cholesky.238 = f32[128,128]{1,0:T(8,128)S(1)} custom-call(f32[128,128]{1,0:T(8,128)S(1)} %cholesky.275), custom_call_target="Cholesky" | custom-call | tf_op jit(solution)/shard_map/jit(cholesky)/cholesky | solution.py:39
  496.6 9.8 custom-call.36
  507.0 11.7 %cholesky.255 = f32[128,128]{1,0:T(8,128)S(1)} custom-call(f32[128,128]{1,0:T(8,128)S(1)} %convolution_subtract_fusion.8), custom_call_target="Cholesky" | custom-call | tf_op jit(solution)/shard_map/jit(cholesky)/cholesky | solution.py:39
  559.2 19.5 %fusion.304 = (f32[128]{0:T(128)S(1)}, f32[128]{0:T(128)S(1)}, f32[128]{0:T(128)S(1)}, f32[128]{0:T(128)S(1)}, f32[128]{0:T(128)S(1)}, /*index=5*/f32[128]{0:T(1...) fusion(f32[128,128]{1,0:T(8,128)S(1)} %select_select_fusion.1, ...), kind=kLoop, calls=%fused_computation.493 | loop fusion | flops 11904 | bytes 32504 | tf_op jit(solution)/shard_map/eval_jaxpr/div | solution.py:76
  583.2 6.6 sort
  589.7 65.7 %while.35 = (s32[]{:T(128)}, f32[128]{0:T(128)S(1)}, f32[3,32,128]{2,1,0:T(8,128)S(1)}, f32[3,32,128]{2,1,0:T(8,128)S(1)}, f32[3,32]{1,0:T(4,128)S(1)}, /*index=...) while((s32[]{:T(128)}, f32[128]{0:T(128)S(1)}, ...), condition=%wide.region_12.13_spmd, body=%wide.region_11.12_spmd.sunk | while | flops 8226 | bytes 101341 | solution.py:76
  591.2 20.3 %fusion.529 = (f32[128]{0:T(128)S(1)}, f32[128]{0:T(128)S(1)}, f32[128]{0:T(128)S(1)}, f32[128]{0:T(128)S(1)}, f32[128]{0:T(128)S(1)}, /*index=5*/f32[128]{0:T(1...) fusion(f32[3,32,128]{2,1,0:T(8,128)S(1)} %get-tuple-element.124, ...), kind=kLoop, calls=%fused_computation.172.clone.1 | loop fusion | flops 8192 | bytes 33536 | tf_op jit(solution)/shard_map/while/body/eval_jaxpr/sub | solution.py:76
  613.1 20.3 %fusion.529 = (f32[128]{0:T(128)S(1)}, f32[128]{0:T(128)S(1)}, f32[128]{0:T(128)S(1)}, f32[128]{0:T(128)S(1)}, f32[128]{0:T(128)S(1)}, /*index=5*/f32[128]{0:T(1...) fusion(f32[3,32,128]{2,1,0:T(8,128)S(1)} %get-tuple-element.124, ...), kind=kLoop, calls=%fused_computation.172.clone.1 | loop fusion | flops 8192 | bytes 33536 | tf_op jit(solution)/shard_map/while/body/eval_jaxpr/sub | solution.py:76
  635.0 20.3 %fusion.529 = (f32[128]{0:T(128)S(1)}, f32[128]{0:T(128)S(1)}, f32[128]{0:T(128)S(1)}, f32[128]{0:T(128)S(1)}, f32[128]{0:T(128)S(1)}, /*index=5*/f32[128]{0:T(1...) fusion(f32[3,32,128]{2,1,0:T(8,128)S(1)} %get-tuple-element.124, ...), kind=kLoop, calls=%fused_computation.172.clone.1 | loop fusion | flops 8192 | bytes 33536 | tf_op jit(solution)/shard_map/while/body/eval_jaxpr/sub | solution.py:76
  657.1 3.2 fusion.368
  660.4 3.3 fusion.367
  663.7 3.0 fusion.366
  666.7 3.4 fusion.365
  670.1 3.3 fusion.364
  673.4 3.3 fusion.363
  676.7 3.1 fusion.362
  679.7 3.2 fusion.361
  682.9 7.0 convolution_bitcast_fusion
  690.1 2.7 copy.144
  692.7 2.5 copy.114
  695.3 5.3 all-to-all-start.1
  700.5 10.8 %while.36 = (s32[]{:T(128)}, f32[512,512]{1,0:T(8,128)S(1)}, s32[4,2]{0,1:T(2,128)S(1)}, f32[4,128,128]{2,1,0:T(8,128)}, s32[]{:T(128)}) while((s32[]{:T(128)}, f32[512,512]{1,0:T(8,128)S(1)}, s32[4,2]{0,1:T(2,128)S(1)}, f32[4,128,128]{2,1,0:T(8,128)}, s32[]{:T(128)}) %tuple.402), condition=%wide.while_cond.1, body=%wide.while_body.1.sunk | while | flops 2 | bytes 132205 | solution.py:40
  706.6 2.0 bitcast_dynamic-update-slice_fusion.8
  711.4 37.8 %all-to-all-done.1 = f32[4,128,8,128]{3,2,0,1:T(8,128)} async-done(((f32[4,128,8,128]{3,2,0,1:T(8,128)}), f32[4,128,8,128]{3,2,0,1:T(8,128)}, u32[]{:S(2)}, u32[]{:S(2)}) %all-to-all-start.1) | async-done | bytes 2097184 | tf_op jit(solution)/shard_map/all_to_all | solution.py:132
  749.1 4.3 copy.118
  753.4 3.3 all_to_all.49
  760.1 3.5 fusion.493
  763.6 7.9 bitcast_add_fusion.2
  773.8 4.4 all-to-all-start.2
  778.2 2.7 fusion.360
  780.9 40.7 %custom-call.37 = f32[4,128,128]{1,2,0:T(8,128)} custom-call(f32[4,128,128]{2,1,0:T(8,128)} %get-tuple-element.177), custom_call_target="InvertDiagBlocksLowerTriangular" | custom-call | tf_op jit(solution)/shard_map/jit(_cho_solve)/triangular_solve | solution.py:40
  821.7 2.7 copy.110
  824.3 121.7 %scatter_custom_fusion = f32[3,131072]{0,1:T(8,128)} fusion(s32[8192]{0:T(1024)} %get-tuple-element.196, f32[]{:T(128)} %constant.319.clone.1, f32[8192,3]{1,0:T(8,128)} %copy.110, s32[8192]{0:T(1024)S(1)} %broadcast_clamp_fusion), kind=kCustom, calls=%fused_computation.235 | custom fusion | flops 24576 | bytes 1573376 | tf_op jit(solution)/shard_map/scatter-add | solution.py:122
  946.0 36.2 %copy.134 = f32[3,2,512,128]{3,2,1,0:T(8,128)} copy(f32[3,2,512,128]{0,3,2,1:T(8,128)} %bitcast.280) | data formatting | bytes 3145728 | tf_op jit(solution)/shard_map/reshape.86
  982.2 2.6 fusion.359
  984.8 2.6 fusion.358
  987.4 2.7 fusion.357
  990.0 2.6 fusion.356
  992.6 2.6 fusion.355
  1002.9 3.3 fusion.226
  1008.5 2.4 bitcast_add_fusion.1
  1010.8 2.5 copy.120
  1013.4 9.7 all-to-all-start.3
  1030.0 3.6 fusion.492
  1033.6 3.7 bitcast_add_fusion.3
  1039.2 12.5 %all-to-all-done.3 = f32[4,128,8,128]{3,2,0,1:T(8,128)} async-done(((f32[4,128,8,128]{3,2,0,1:T(8,128)}), f32[4,128,8,128]{3,2,0,1:T(8,128)}, u32[]{:S(2)}, u32[]{:S(2)}) %all-to-all-start.3) | async-done | bytes 2097184 | tf_op jit(solution)/shard_map/all_to_all | solution.py:144
  1051.7 3.1 bitcast_add_fusion
  (217 shorter events, 66.6 us)
Async XLA Ops:
  4.9 685.2 %all-to-all-start = ((f32[4,2,512,128]{3,0,1,2:T(4,128)}), f32[4,2,512,128]{3,0,1,2:T(4,128)}, u32[]{:S(2)}, u32[]{:S(2)}) async-start(f32[4,2,512,128]{3,0,1,2:T(4,128)} %copy.112), calls=%async_computation | async-start | bytes 4194304 | tf_op jit(solution)/shard_map/all_to_all | solution.py:126
  15.4 0.8 copy-start.12
  15.4 1.4 slice-start
  166.0 3.6 copy-start.13
  166.0 3.6 copy-start.11
  166.0 3.6 copy-start.14
  170.5 2.7 copy-start.15
  227.0 810.8 %collective-permute-start.3 = (f32[6,256]{1,0:T(8,128)S(1)}, f32[6,256]{1,0:T(8,128)}, u32[]{:S(2)}, u32[]{:S(2)}) collective-permute-start(f32[6,256]{1,0:T(8,128)S(1)} %bitcast.1866), channel_id=1, source_target_pairs={{1,0},{2,1},{3,2},{0,3},{5,4},{6,5},{7,6},{4,7},{9,8},{10,9},{11,1... | collective-permute-start | bytes 18440 | tf_op jit(solution)/shard_map/ppermute | solution.py:24
  231.8 806.0 %collective-permute-start.2 = (f32[6,256]{1,0:T(8,128)}, f32[6,256]{1,0:T(8,128)}, u32[]{:S(2)}, u32[]{:S(2)}) collective-permute-start(f32[6,256]{1,0:T(8,128)} %bitcast.571), channel_id=1, source_target_pairs={{3,0},{0,1},{1,2},{2,3},{7,4},{4,5},{5,6},{6,7},{11,8},{8,9},{9,10... | collective-permute-start | bytes 18440 | tf_op jit(solution)/shard_map/ppermute | solution.py:24
  232.5 805.3 %collective-permute-start.1 = (f32[6,256]{1,0:T(8,128)}, f32[6,256]{1,0:T(8,128)}, u32[]{:S(2)}, u32[]{:S(2)}) collective-permute-start(f32[6,256]{1,0:T(8,128)} %bitcast.569), channel_id=1, source_target_pairs={{4,0},{8,4},{12,8},{16,12},{20,16},{24,20},{28,24},{32,28},{36,32}... | collective-permute-start | bytes 18440 | tf_op jit(solution)/shard_map/ppermute | solution.py:18
  238.4 799.4 %collective-permute-start = (f32[6,256]{1,0:T(8,128)}, f32[6,256]{1,0:T(8,128)}, u32[]{:S(2)}, u32[]{:S(2)}) collective-permute-start(f32[6,256]{1,0:T(8,128)} %bitcast.567), channel_id=1, source_target_pairs={{0,4},{4,8},{8,12},{12,16},{16,20},{20,24},{24,28},{28,32},{32,36}... | collective-permute-start | bytes 18440 | tf_op jit(solution)/shard_map/ppermute | solution.py:18
  436.1 219.3 %copy-start.10 = (f32[3,32,128]{2,1,0:T(8,128)}, f32[3,32,128]{2,1,0:T(8,128)S(1)}, u32[]{:S(2)}) copy-start(f32[3,32,128]{2,1,0:T(8,128)S(1)} %get-tuple-element.164) | copy-start | bytes 147460
  695.3 5.3 copy-start.26
  695.3 53.8 %all-to-all-start.1 = ((f32[4,128,8,128]{3,2,0,1:T(8,128)}), f32[4,128,8,128]{3,2,0,1:T(8,128)}, u32[]{:S(2)}, u32[]{:S(2)}) async-start(f32[4,128,8,128]{3,2,0,1:T(8,128)} %copy.114), calls=%async_computation.1 | async-start | bytes 4194304 | tf_op jit(solution)/shard_map/all_to_all | solution.py:132
  756.6 2.2 copy-start.8
  758.5 1.6 copy-start.1
  760.1 3.5 copy-start.16
  773.8 232.4 %all-to-all-start.2 = ((f32[4,4,32,8,128]{4,2,3,1,0:T(8,128)}), f32[4,4,32,8,128]{4,2,3,1,0:T(8,128)}, u32[]{:S(2)}, u32[]{:S(2)}) async-start(f32[4,4,32,8,128]{4,2,3,1,0:T(8,128)} %pad_maximum_fusion), calls=%async_computation.2 | async-start | bytes 4194304 | tf_op jit(solution)/shard_map/all_to_all | solution.py:135
  946.0 51.2 %copy-start.17 = (f32[1,128]{1,0:T(1,128)S(1)}, f32[1,128]{1,0:T(1,128)}, u32[]{:S(2)}) copy-start(f32[1,128]{1,0:T(1,128)} %get-tuple-element.299) | copy-start | bytes 1540
  946.0 51.2 %copy-start.18 = (f32[1,128]{1,0:T(1,128)S(1)}, f32[1,128]{1,0:T(1,128)}, u32[]{:S(2)}) copy-start(f32[1,128]{1,0:T(1,128)} %get-tuple-element.301) | copy-start | bytes 1540
  946.0 51.2 %copy-start.19 = (f32[1,128]{1,0:T(1,128)S(1)}, f32[1,128]{1,0:T(1,128)}, u32[]{:S(2)}) copy-start(f32[1,128]{1,0:T(1,128)} %get-tuple-element.303) | copy-start | bytes 1540
  946.0 51.2 %copy-start.20 = (f32[1,128]{1,0:T(1,128)S(1)}, f32[1,128]{1,0:T(1,128)}, u32[]{:S(2)}) copy-start(f32[1,128]{1,0:T(1,128)} %get-tuple-element.305) | copy-start | bytes 1540
  946.0 51.2 %copy-start.21 = (f32[1,128]{1,0:T(1,128)S(1)}, f32[1,128]{1,0:T(1,128)}, u32[]{:S(2)}) copy-start(f32[1,128]{1,0:T(1,128)} %get-tuple-element.307) | copy-start | bytes 1540
  946.0 51.2 %copy-start.22 = (f32[1,128]{1,0:T(1,128)S(1)}, f32[1,128]{1,0:T(1,128)}, u32[]{:S(2)}) copy-start(f32[1,128]{1,0:T(1,128)} %get-tuple-element.309) | copy-start | bytes 1540
  946.0 51.2 %copy-start.23 = (f32[1,128]{1,0:T(1,128)S(1)}, f32[1,128]{1,0:T(1,128)}, u32[]{:S(2)}) copy-start(f32[1,128]{1,0:T(1,128)} %get-tuple-element.311) | copy-start | bytes 1540
  946.0 51.2 %copy-start.24 = (f32[1,128]{1,0:T(1,128)S(1)}, f32[1,128]{1,0:T(1,128)}, u32[]{:S(2)}) copy-start(f32[1,128]{1,0:T(1,128)} %get-tuple-element.313) | copy-start | bytes 1540
  946.0 51.2 %copy-start.25 = (f32[1,128]{1,0:T(1,128)S(1)}, f32[1,128]{1,0:T(1,128)}, u32[]{:S(2)}) copy-start(f32[1,128]{1,0:T(1,128)} %get-tuple-element.315) | copy-start | bytes 1540
  998.1 1.4 copy-start.4
  1006.2 2.2 copy-start.2
  1006.2 2.3 copy-start.7
  1013.4 9.7 copy-start.5
  1013.4 9.7 copy-start.6
  1013.4 10.1 copy-start.9
  1013.4 38.3 %all-to-all-start.3 = ((f32[4,128,8,128]{3,2,0,1:T(8,128)}), f32[4,128,8,128]{3,2,0,1:T(8,128)}, u32[]{:S(2)}, u32[]{:S(2)}) async-start(f32[4,128,8,128]{3,2,0,1:T(8,128)} %copy.120), calls=%async_computation.3 | async-start | bytes 4194304 | tf_op jit(solution)/shard_map/all_to_all | solution.py:144
  1027.0 2.9 copy-start
  1033.6 3.7 copy-start.3
